TPU v7x, 32 devices: a whole 2x2x4 slice. The times are simulated.
32 devices in a mesh: head: 8 (over y, x, core), key: 4 (over z).
Axes of the slice: x: 2, y: 2, z: 4, core: 2. Of those that a mesh axis runs over, the one named last changes fastest.
Arguments:
- queries: bfloat16 [128, 128, 192], P(None, 'head'), may hold values from -16 to 16
- w_uk: bfloat16 [128, 128, 512], P('head'), may hold values from -0.5 to 0.5
- w_uv: bfloat16 [128, 512, 128], P('head'), may hold values from -0.25 to 0.25
- latent: bfloat16 [8192, 576], P('key'), may hold values from -5 to 5
- out_grad: bfloat16 [128, 128, 128], P(None, 'head'), may hold values from -6 to 6
- offsets: int32 [128], replicated, may hold values from 2048 to 8191, as said below
Outputs:
- d_queries: bfloat16 [128, 128, 192], P('key', 'head')
- d_latent: bfloat16 [8192, 576], P('key')
Inputs may be any that keep to these rules, and one draw needn't show every extreme that they name: Row r sees keys 0 to offsets[r].
All inputs are finite; a program needn't handle non-finite values.
Results may differ from a plain program's by a relative error of at most 0.0079.
Values may be sent and summed in bfloat16 or wider, within the bound.
A program may use at most 128 MiB of HBM per device.

v0:
```python
import math

import jax
import jax.numpy as jnp
from jax import lax
from jax.sharding import PartitionSpec as P

floor_score = -1e30


def joined(part, axis, combine):
    gathered = jax.tree.map(lambda a: lax.all_gather(a, axis), part)

    def take(source):
        return jax.tree.map(lambda a: lax.dynamic_index_in_dim(a, source, 0, False), gathered)

    return lax.fori_loop(
        1, lax.axis_size(axis), lambda source, state: combine(state, take(source)), take(0)
    )


def combine_norms(earlier, later):
    top = jnp.maximum(earlier[0], later[0])
    total = earlier[1] * jnp.exp(earlier[0] - top) + later[1] * jnp.exp(later[0] - top)
    return (top, total)


def shards(queries, w_uk, w_uv, latent, out_grad, offsets):
    rows, heads, width = queries.shape
    keys = latent.shape[0]
    nope_width = w_uk.shape[1]
    lat_width = w_uk.shape[2]
    scale = 1.0 / math.sqrt(width)
    q_lat = jnp.einsum(
        "rhd,hdc->rhc", queries[:, :, :nope_width], w_uk, preferred_element_type=jnp.float32
    ).astype(jnp.bfloat16)
    q_cat = jnp.concatenate([q_lat, queries[:, :, nope_width:]], axis=2)
    d_lat = jnp.einsum("rhe,hce->rhc", out_grad, w_uv, preferred_element_type=jnp.float32).astype(
        jnp.bfloat16
    )
    scores = jnp.einsum("rhc,kc->hrk", q_cat, latent, preferred_element_type=jnp.float32) * scale
    position = lax.axis_index("key") * keys + jnp.arange(keys, dtype=jnp.int32)
    visible = (position[None, :] <= offsets[:, None])[None]
    masked = jnp.where(visible, scores, floor_score)
    local_top = jnp.max(masked, axis=2)
    local_total = jnp.sum(jnp.where(visible, jnp.exp(masked - local_top[..., None]), 0.0), axis=2)
    top, total = joined((local_top, local_total), "key", combine_norms)
    log_norm = top + jnp.log(total)
    probs = jnp.where(visible, jnp.exp(masked - log_norm[..., None]), 0.0)
    d_probs = jnp.einsum(
        "rhc,kc->hrk", d_lat, latent[:, :lat_width], preferred_element_type=jnp.float32
    )
    delta = lax.psum(jnp.sum(probs * d_probs, axis=2), "key")
    d_scores = (probs * (d_probs - delta[..., None])).astype(jnp.bfloat16)
    probs_b = probs.astype(jnp.bfloat16)
    up_key = w_uk.astype(jnp.float32)
    part_sum = (
        jnp.einsum("hrk,kc->rhc", d_scores, latent, preferred_element_type=jnp.float32) * scale
    )
    nope = jnp.einsum(
        "rhc,hdc->rhd", part_sum[..., :lat_width], up_key, precision=lax.Precision.HIGHEST
    )
    dq_sum = lax.psum_scatter(
        jnp.concatenate([nope, part_sum[..., lat_width:]], axis=2),
        "key",
        scatter_dimension=0,
        tiled=True,
    )
    d_queries = dq_sum.astype(jnp.bfloat16)
    from_scores = (
        jnp.einsum("hrk,rhc->kc", d_scores, q_cat, preferred_element_type=jnp.float32) * scale
    )
    from_values = jnp.einsum("hrk,rhc->kc", probs_b, d_lat, preferred_element_type=jnp.float32)
    d_latent = lax.psum(
        jnp.concatenate(
            [from_scores[:, :lat_width] + from_values, from_scores[:, lat_width:]], axis=1
        ),
        "head",
    ).astype(jnp.bfloat16)
    return (d_queries, d_latent)


def solution(mesh):
    return jax.shard_map(
        shards,
        mesh=mesh,
        in_specs=(
            P(None, "head", None),
            P("head", None, None),
            P("head", None, None),
            P("key", None),
            P(None, "head", None),
            P(),
        ),
        out_specs=(P("key", "head", None), P("key", None)),
        check_vma=False,
    )
```

profile of v0, /device:TPU:0, one launch (start us, length us, event | category | flops | bytes accessed | tf_op | source)
XLA Modules:
  0.0 233.1 jit_solution(15037375372007042544)
XLA Ops:
  7.2 0.0 reduce-scatter.2.cloned.1.call-start
  7.3 1.1 slice.24
  8.4 0.4 copy-done
  8.8 1.8 convert_bitcast_fusion
  10.7 0.2 broadcast_compare_fusion
  10.9 8.4 %bitcast_reduce_fusion = (f32[16,128]{1,0:T(8,128)S(1)}, f32[128,16,2048]{2,0,1:T(8,128)S(1)}) fusion(pred[128,2048]{1,0:T(8,128)(4,1)S(1)} %broadcast_compare_fusion, bf16[2048,576]{0,1:T(8,128)(2,1)S(1)} %copy-done.9, bf16[128,16,64]{0,2,1:T(8,128)(2,1)S(1)} %slice.24, bf16[128,16,512]{0,2,1:T(8,128)(2,1)S(1)} %convert_bitcast_fusion), kind=kOutput, calls=%fused_computation.12 | convolution fusion | flops 4849137664 | bytes 21766144 | tf_op jit(solution)/shard_map/rhc,kc->hrk/dot_general | solution.py:41
  19.3 14.8 %all-gather = f32[64,128]{1,0:T(8,128)S(1)} all-gather(f32[16,128]{1,0:T(8,128)S(1)} %get-tuple-element.151), channel_id=2, replica_groups=mesh['head'=8,'key'=4] {'key'}, dimensions={0}, use_global_device_ids=true | all-gather | bytes 40960 | tf_op jit(solution)/shard_map/all_gather | solution.py:12
  34.1 5.0 %fusion.7 = f32[16,128]{1,0:T(8,128)S(1)} fusion(f32[128,16,2048]{2,0,1:T(8,128)S(1)} %get-tuple-element.152, f32[16,128]{1,0:T(8,128)S(1)} %get-tuple-element.151, pred[128,2048]{1,0:T(8,128)(4,1)S(1)} %broadcast_compare_fusion), kind=kLoop, calls=%fused_computation.15 | loop fusion | flops 20969472 | bytes 17055744 | tf_op jit(solution)/shard_map/reduce_sum | solution.py:46
  39.2 13.3 %all-gather.1 = f32[64,128]{1,0:T(8,128)S(1)} all-gather(f32[16,128]{1,0:T(8,128)S(1)} %fusion.7), channel_id=3, replica_groups=mesh['head'=8,'key'=4] {'key'}, dimensions={0}, use_global_device_ids=true | all-gather | bytes 40960 | tf_op jit(solution)/shard_map/all_gather | solution.py:12
  52.6 0.1 while.17
  52.7 2.5 %convolution_convert_fusion = bf16[16,512,128]{2,1,0:T(8,128)(2,1)S(1)} fusion(bf16[16,512,128]{2,1,0:T(8,128)(2,1)} %param.10, bf16[128,16,128]{2,1,0:T(8,128)(2,1)S(1)} %copy-done.7), kind=kOutput, calls=%fused_computation.38 | convolution fusion | flops 269484032 | bytes 4718592 | tf_op jit(solution)/shard_map/rhe,hce->rhc/dot_general | solution.py:38
  55.2 16.4 %fusion.2 = (f32[16,128]{1,0:T(8,128)S(1)}, f32[128,16,2048]{2,0,1:T(8,128)}) fusion(f32[16,128]{1,0:T(8,128)S(1)} %log_add_fusion, f32[128,16,2048]{2,0,1:T(8,128)} %copy-done.2, pred[128,2048]{1,0:T(8,128)(4,1)S(1)} %broadcast_compare_fusion, bf16[2048,576]{0,1:T(8,128)(2,1)S(1)} %copy-done.10, bf16[16,512,128]{2,1,0:T(8,128)(2,1)S(1)} %convolution_convert_fusion), kind=kOutput, calls=%fused_computation.7 | convolution fusion | flops 4320131072 | bytes 38289408 | tf_op jit(solution)/shard_map/rhc,kc->hrk/dot_general | solution.py:50
  71.6 11.8 %psum.14 = f32[16,128]{1,0:T(8,128)S(1)} all-reduce(f32[16,128]{1,0:T(8,128)S(1)} %get-tuple-element.153), channel_id=1, replica_groups=mesh['head'=8,'key'=4] {'key'}, use_global_device_ids=true, to_apply=%region_5.6 | all-reduce | flops 2048 | bytes 16384 | tf_op jit(solution)/shard_map/psum | solution.py:53
  83.5 13.1 %fusion.4 = bf16[16,128,2048]{2,1,0:T(8,128)(2,1)S(1)} fusion(f32[128,16,2048]{2,0,1:T(8,128)} %get-tuple-element.154, f32[16,128]{1,0:T(8,128)S(1)} %psum.14, f32[16,128]{1,0:T(8,128)S(1)} %log_add_fusion, f32[128,16,2048]{2,0,1:T(8,128)} %copy-done.2, pred[128,2048]{1,0:T(8,128)(4,1)S(1)} %broadcast_compare_fusion), kind=kLoop, calls=%fused_computation.9 | loop fusion | flops 29360128 | bytes 42221568 | tf_op jit(solution)/shard_map/convert_element_type | solution.py:54
  96.6 5.1 %multiply_bitcast_fusion = f32[128,16,576]{0,2,1:T(8,128)S(1)} fusion(bf16[16,128,2048]{2,1,0:T(8,128)(2,1)S(1)} %fusion.4, bf16[2048,576]{0,1:T(8,128)(2,1)S(1)} %copy-done.11), kind=kOutput, calls=%fused_computation.23 | convolution fusion | flops 4833017856 | bytes 15466496 | tf_op jit(solution)/shard_map/hrk,kc->rhc/dot_general | solution.py:58
  101.8 2.5 %fusion.28 = f32[128,16,128]{0,2,1:T(8,128)S(1)} fusion(bf16[16,128,512]{2,1,0:T(8,128)(2,1)S(1)} %copy-done, f32[128,16,576]{0,2,1:T(8,128)S(1)} %multiply_bitcast_fusion), kind=kOutput, calls=%fused_computation.40 | convolution fusion | flops 1610612736 | bytes 7340032 | tf_op jit(solution)/shard_map/rhc,hdc->rhd/dot_general | solution.py:60
  104.3 0.1 pad_maximum_fusion.2
  104.4 2.0 copy.21
  106.4 0.0 reduce-scatter.2.cloned.1.call-update
  106.5 8.3 %bitcast_multiply_fusion.2 = f32[2048,576]{0,1:T(8,128)S(1)} fusion(bf16[16,128,2048]{2,1,0:T(8,128)(2,1)} %copy-done.3, bf16[128,16,64]{0,2,1:T(8,128)(2,1)S(1)} %slice.24, bf16[128,16,512]{0,2,1:T(8,128)(2,1)} %copy-done.4), kind=kOutput, calls=%fused_computation.22 | convolution fusion | flops 4837736448 | bytes 15466496 | tf_op jit(solution)/shard_map/hrk,rhc->kc/dot_general | solution.py:71
  114.7 9.0 %slice_add_fusion = f32[2048,512]{0,1:T(8,128)S(1)} fusion(f32[2048,576]{0,1:T(8,128)S(1)} %bitcast_multiply_fusion.2, f32[16,128]{1,0:T(8,128)S(1)} %log_add_fusion, f32[128,16,2048]{2,0,1:T(8,128)} %copy-done.2, pred[128,2048]{1,0:T(8,128)(4,1)S(1)} %broadcast_compare_fusion, bf16[16,512,128]{2,1,0:T(8,128)(2,1)S(1)} %copy-done.6), kind=kOutput, calls=%fused_computation.24 | convolution fusion | flops 4316987392 | bytes 27795456 | tf_op jit(solution)/shard_map/hrk,rhc->kc/dot_general | solution.py:73
  123.8 2.4 %pad_maximum_fusion = f32[2048,576]{0,1:T(8,128)} fusion(f32[2048,64]{0,1:T(8,128)S(1)} %slice.37, f32[2048,512]{0,1:T(8,128)S(1)} %slice_add_fusion), kind=kLoop, calls=%fused_computation.21 | loop fusion | flops 1179648 | bytes 9437184 | tf_op jit(solution)/shard_map/concatenate | solution.py:75
  126.2 98.2 %all-reduce.1 = bf16[2048,576]{0,1:T(8,128)(2,1)} all-reduce(f32[2048,576]{0,1:T(8,128)} %pad_maximum_fusion), channel_id=1, replica_groups=mesh['head'=8,'key'=4] {'head'}, use_global_device_ids=true, to_apply=%region_7.8 | all-reduce | flops 1179648 | bytes 7077888 | tf_op jit(solution)/shard_map/psum | solution.py:74
  224.5 1.8 convert_element_type.30
  (33 shorter events, 0.2 us)
Async XLA Ops:
  7.2 1.7 copy-start
  7.2 3.5 %copy-start.8 = (s32[128]{0:T(128)S(1)}, s32[128]{0:T(128)}, u32[]{:S(2)}) copy-start(s32[128]{0:T(128)} %param.13) | copy-start | bytes 1540
  7.2 217.3 %reduce-scatter.2.cloned.1.call-start = ((), (), s32[]{:S(2)}) async-start(), calls=%async_computation.1 | async-start | bytes 2621440 | tf_op jit(solution)/shard_map/reduce_scatter | solution.py:63
  7.2 3.7 %copy-start.9 = (bf16[2048,576]{0,1:T(8,128)(2,1)S(1)}, bf16[2048,576]{0,1:T(8,128)(2,1)}, u32[]{:S(2)}) copy-start(bf16[2048,576]{0,1:T(8,128)(2,1)} %param.11) | copy-start | bytes 7077892
  10.7 8.6 %copy-start.4 = (bf16[128,16,512]{0,2,1:T(8,128)(2,1)}, bf16[128,16,512]{0,2,1:T(8,128)(2,1)S(1)}, u32[]{:S(2)}) copy-start(bf16[128,16,512]{0,2,1:T(8,128)(2,1)S(1)} %convert_bitcast_fusion) | copy-start | bytes 6291460
  19.3 19.9 %copy-start.2 = (f32[128,16,2048]{2,0,1:T(8,128)}, f32[128,16,2048]{2,0,1:T(8,128)S(1)}, u32[]{:S(2)}) copy-start(f32[128,16,2048]{2,0,1:T(8,128)S(1)} %get-tuple-element.152) | copy-start | bytes 50331652
  34.1 18.5 %copy-start.7 = (bf16[128,16,128]{2,1,0:T(8,128)(2,1)S(1)}, bf16[128,16,128]{2,1,0:T(8,128)(2,1)}, u32[]{:S(2)}) copy-start(bf16[128,16,128]{2,1,0:T(8,128)(2,1)} %param.12) | copy-start | bytes 1572868
  52.7 2.5 %copy-start.10 = (bf16[2048,576]{0,1:T(8,128)(2,1)S(1)}, bf16[2048,576]{0,1:T(8,128)(2,1)}, u32[]{:S(2)}) copy-start(bf16[2048,576]{0,1:T(8,128)(2,1)} %param.11) | copy-start | bytes 7077892
  55.2 16.5 %copy-start.5 = (bf16[16,512,128]{2,1,0:T(8,128)(2,1)}, bf16[16,512,128]{2,1,0:T(8,128)(2,1)S(1)}, u32[]{:S(2)}) copy-start(bf16[16,512,128]{2,1,0:T(8,128)(2,1)S(1)} %convolution_convert_fusion) | copy-start | bytes 6291460
  83.5 13.2 %copy-start.11 = (bf16[2048,576]{0,1:T(8,128)(2,1)S(1)}, bf16[2048,576]{0,1:T(8,128)(2,1)}, u32[]{:S(2)}) copy-start(bf16[2048,576]{0,1:T(8,128)(2,1)} %param.11) | copy-start | bytes 7077892
  96.6 5.1 %copy-start.3 = (bf16[16,128,2048]{2,1,0:T(8,128)(2,1)}, bf16[16,128,2048]{2,1,0:T(8,128)(2,1)S(1)}, u32[]{:S(2)}) copy-start(bf16[16,128,2048]{2,1,0:T(8,128)(2,1)S(1)} %fusion.4) | copy-start | bytes 25165828
  106.5 8.3 %copy-start.6 = (bf16[16,512,128]{2,1,0:T(8,128)(2,1)S(1)}, bf16[16,512,128]{2,1,0:T(8,128)(2,1)}, u32[]{:S(2)}) copy-start(bf16[16,512,128]{2,1,0:T(8,128)(2,1)} %copy-done.5) | copy-start | bytes 6291460
  123.8 102.5 %copy-start.1 = (bf16[16,128,512]{2,1,0:T(8,128)(2,1)S(1)}, bf16[16,128,512]{2,1,0:T(8,128)(2,1)}, u32[]{:S(2)}) copy-start(bf16[16,128,512]{2,1,0:T(8,128)(2,1)} %param.9) | copy-start | bytes 6291460
Sparse Core Ops, SparseCore 0:
  106.6 41.8 reduce-scatter.1
where the time goes:
time: 233 us
  blocking collectives  138 us (59%)
  matrix products  53.9 us (23%)
  other arithmetic  22.8 us (10%)
  between operations  14.3 us (6%)
  local copies, waits for them, and re-layouts  3.72 us (2%)
    psum x1, blocking collectives, shards(): lax.psum(jnp.concatenate([from_scores[:, :lat_width] + from_values, from_...  98.2 us
    all_gather x2, blocking collectives, joined(): gathered = jax.tree.map(lambda a: lax.all_gather(a, axis), part)  28.2 us
    dot_general x1, matrix products, shards(): jnp.einsum('rhc,kc->hrk', d_lat, latent[:, :lat_width], preferred_element...  16.4 us
    convert_element_type x1, other arithmetic, shards(): d_scores = (probs * (d_probs - delta[..., None])).astype(jnp.bfloat16)  13.1 us
    psum x1, blocking collectives, shards(): delta = lax.psum(jnp.sum(probs * d_probs, axis=2), 'key')  11.8 us
    dot_general x1, matrix products, shards(): jnp.einsum('hrk,rhc->kc', probs_b, d_lat, preferred_element_type=jnp.floa...  9.01 us
    dot_general x1, matrix products, shards(): jnp.einsum('rhc,kc->hrk', q_cat, latent, preferred_element_type=jnp.float32)  8.36 us
    dot_general x1, matrix products, shards(): jnp.einsum('hrk,rhc->kc', d_scores, q_cat, preferred_element_type=jnp.flo...  8.25 us
  transfers between devices with their start and end apart: 1, of which 0 were waited for; matrix products, arithmetic and copies ran while one was open for 8% of the time, Pallas kernels for 0%

commit v1 on v0

v1 whole, which is shorter than its diff:
```python
import functools
import math

import jax
import jax.numpy as jnp
from jax import lax
from jax.experimental import pallas as pl
from jax.experimental.pallas import tpu as pltpu
from jax.sharding import PartitionSpec as P

floor_score = -1e30
MESH = pl.DeviceIdType.MESH
f32 = jnp.float32
bf16 = jnp.bfloat16
VMEM_BYTES = 60 * 1024 * 1024


def dot(a, b):
    return lax.dot_general(a, b, (((1,), (0,)), ((), ())), preferred_element_type=f32)


def dot_t(a, b):
    return lax.dot_general(a, b, (((1,), (1,)), ((), ())), preferred_element_type=f32)


def scores_kernel(
    scale, group, tile, q_ref, og_ref, uk_ref, uv_ref, lat_ref, off_ref,
    e_ref, dp_ref, qc_ref, dl_ref, st_ref, s_ref,
):
    step = pl.program_id(0)
    rows = q_ref.shape[1]
    nope = uk_ref.shape[1]
    width = uk_ref.shape[2]
    keys = lat_ref.shape[0]
    for h in range(group):
        at = pl.ds(h * rows, rows)
        qc_ref[at, :width] = dot(q_ref[h, :, :nope], uk_ref[h]).astype(bf16)
        qc_ref[at, width:] = q_ref[h, :, nope:]
        dl_ref[at, :] = dot_t(og_ref[h], uv_ref[h]).astype(bf16)
    qc = qc_ref[...]
    dl = dl_ref[...]
    off = jnp.concatenate([off_ref[...]] * group, axis=1)
    top = jnp.full((1, group * rows), floor_score, f32)
    for t in range(keys // tile):
        at = pl.ds(t * tile, tile)
        s = dot_t(lat_ref[at, :], qc) * scale
        position = lax.broadcasted_iota(jnp.int32, s.shape, 0) + t * tile
        s = jnp.where(position <= off, s, floor_score)
        s_ref[at, :] = s
        top = jnp.maximum(top, jnp.max(s, axis=0, keepdims=True))
        dp_ref[at, :] = dot_t(lat_ref[at, :width], dl).astype(bf16)
    shift = jnp.maximum(top, 0.5 * floor_score)
    total = jnp.zeros((1, group * rows), f32)
    acc = jnp.zeros((1, group * rows), f32)
    for t in range(keys // tile):
        at = pl.ds(t * tile, tile)
        e = jnp.exp(s_ref[at, :] - shift).astype(bf16)
        e_ref[at, :] = e
        e = e.astype(f32)
        total = total + jnp.sum(e, axis=0, keepdims=True)
        acc = acc + jnp.sum(e * dp_ref[at, :].astype(f32), axis=0, keepdims=True)
    for h in range(group):
        cut = slice(h * rows, (h + 1) * rows)
        at = pl.ds(step * group + h, 1)
        st_ref[0, at, :] = shift[:, cut]
        st_ref[1, at, :] = total[:, cut]
        st_ref[2, at, :] = acc[:, cut]


def stats_kernel(key_n, st_ref, out_ref, got_ref, send_sem, recv_sem):
    me = lax.axis_index("key")
    barrier = pltpu.get_barrier_semaphore()
    for d in range(1, key_n):
        pl.semaphore_signal(
            barrier, inc=1, device_id={"key": lax.rem(me + d, key_n)}, device_id_type=MESH
        )
    pl.semaphore_wait(barrier, key_n - 1)
    copies = []
    for d in range(1, key_n):
        copy = pltpu.make_async_remote_copy(
            src_ref=st_ref,
            dst_ref=got_ref.at[d - 1],
            send_sem=send_sem.at[d - 1],
            recv_sem=recv_sem.at[d - 1],
            device_id={"key": lax.rem(me + d, key_n)},
            device_id_type=MESH,
        )
        copy.start()
        copies.append(copy)
    for copy in copies:
        copy.wait()
    mine = st_ref[0]
    top = mine
    for d in range(key_n - 1):
        top = jnp.maximum(top, got_ref[d, 0])
    near = jnp.exp(mine - top)
    total = near * st_ref[1]
    acc = near * st_ref[2]
    for d in range(key_n - 1):
        part = jnp.exp(got_ref[d, 0] - top)
        total = total + part * got_ref[d, 1]
        acc = acc + part * got_ref[d, 2]
    out_ref[0] = near / total
    out_ref[1] = acc / total


def grads_kernel(
    scale, key_n, rows, tile, e_ref, dp_ref, norm_ref, delta_ref, qc_ref, dl_ref, lt_ref, uk_ref,
    dlat_ref, dq_ref, ds_ref, p_ref, acc_ref,
):
    step = pl.program_id(0)
    width = dl_ref.shape[1]
    nope = uk_ref.shape[1]
    wide = e_ref.shape[1]
    for t in range(wide // tile):
        cut = slice(t * tile, (t + 1) * tile)
        p = e_ref[:, cut].astype(f32) * norm_ref[:, cut]
        p_ref[:, cut] = p.astype(bf16)
        ds_ref[:, cut] = (p * (dp_ref[:, cut].astype(f32) - delta_ref[:, cut])).astype(bf16)
        part = dot(lt_ref[...], ds_ref[:, cut])

        @pl.when(step == 0)
        def _():
            acc_ref[:, cut] = part

        @pl.when(step > 0)
        def _():
            acc_ref[:, cut] += part

    from_scores = dot(ds_ref[...], qc_ref[...]) * scale
    from_values = dot(p_ref[...], dl_ref[...])
    dlat_ref[:, :width] = (from_scores[:, :width] + from_values).astype(bf16)
    dlat_ref[:, width:] = from_scores[:, width:].astype(bf16)

    @pl.when(step == pl.num_programs(0) - 1)
    def _():
        chunk = rows // key_n
        for h in range(wide // rows):
            cut = slice(h * rows, (h + 1) * rows)
            x = acc_ref[:width, cut] * scale
            high = x.astype(bf16)
            low = (x - high.astype(f32)).astype(bf16)
            w = uk_ref[h]
            a = (dot(w, high) + dot(w, low)).T
            b = (acc_ref[width:, cut] * scale).T
            for j in range(key_n):
                at = slice(j * chunk, (j + 1) * chunk)
                dq_ref[j, h, :, :nope] = a[at].astype(bf16)
                dq_ref[j, h, :, nope:] = b[at].astype(bf16)


def joins_kernel(
    key_n, head_n, dlat_ref, dq_ref, out_ref, dqo_ref, work_ref, got_ref, dqg_ref,
    rs_send, rs_recv, ag_send, ag_recv, q_send, q_recv,
):
    mk = lax.axis_index("key")
    mh = lax.axis_index("head")
    bits = head_n.bit_length() - 1
    keys = dlat_ref.shape[0]

    def bit(b):
        return lax.rem(lax.div(mh, 1 << b), 2)

    def partner(b):
        return mh + (1 - 2 * bit(b)) * (1 << b)

    barrier = pltpu.get_barrier_semaphore()
    for d in range(1, key_n):
        pl.semaphore_signal(
            barrier, inc=1, device_id={"key": lax.rem(mk + d, key_n)}, device_id_type=MESH
        )
    for b in range(bits):
        pl.semaphore_signal(
            barrier, inc=1, device_id={"head": partner(b)}, device_id_type=MESH
        )
    pl.semaphore_wait(barrier, key_n - 1 + bits)

    def remote(src, dst, send, recv, where):
        copy = pltpu.make_async_remote_copy(
            src_ref=src, dst_ref=dst, send_sem=send, recv_sem=recv,
            device_id=where, device_id_type=MESH,
        )
        copy.start()
        return copy

    q_copies = []
    for d in range(1, key_n):
        to = lax.rem(mk + d, key_n)
        q_copies.append(
            remote(dq_ref.at[to], dqg_ref.at[d - 1], q_send.at[d - 1], q_recv.at[d - 1], {"key": to})
        )
    orders = [[0] + list(range(1, bits)), [0] + list(range(bits - 1, 0, -1))]
    base = [0, keys // 2]
    place = [0, keys // 2]
    length = keys // 2
    for i in range(bits):
        half = length // 2
        copies = []
        source = dlat_ref if i == 0 else work_ref
        for s in range(2):
            b = orders[s][i]
            v = bit(b)
            away = pl.multiple_of(base[s] + (1 - v) * half, half)
            copies.append(
                remote(
                    source.at[pl.ds(away, half)], got_ref.at[pl.ds(place[s], half)],
                    rs_send.at[s, i], rs_recv.at[s, i], {"head": partner(b)},
                )
            )
            base[s] = pl.multiple_of(base[s] + v * half, half)
        for s in range(2):
            copies[s].wait()
            kept = pl.ds(base[s], half)
            summed = source[kept, :].astype(f32) + got_ref[pl.ds(place[s], half), :].astype(f32)
            if i == bits - 1:
                out_ref[kept, :] = summed.astype(bf16)
            else:
                work_ref[kept, :] = summed.astype(bf16)
            place[s] = place[s] + half
        length = half
    for i in range(bits - 1, -1, -1):
        copies = []
        for s in range(2):
            b = orders[s][i]
            at = pl.ds(base[s], length)
            copies.append(
                remote(
                    out_ref.at[at], out_ref.at[at],
                    ag_send.at[s, i], ag_recv.at[s, i], {"head": partner(b)},
                )
            )
        for s in range(2):
            copies[s].wait()
            base[s] = pl.multiple_of(base[s] - bit(orders[s][i]) * length, length)
        length = 2 * length
    for copy in q_copies:
        copy.wait()
    summed = dq_ref[mk].astype(f32)
    for d in range(key_n - 1):
        summed = summed + dqg_ref[d].astype(f32)
    dqo_ref[...] = summed.astype(bf16)


def vmem(shape=None, index=None):
    return pl.BlockSpec(shape, index, memory_space=pltpu.VMEM)


def shards(key_n, head_n, queries, w_uk, w_uv, latent, out_grad, offsets):
    rows, heads, width = queries.shape
    keys, full = latent.shape
    nope = w_uk.shape[1]
    lat = w_uk.shape[2]
    values = out_grad.shape[2]
    scale = 1.0 / math.sqrt(width)
    wide = heads * rows
    group = 4 if heads % 4 == 0 else heads
    span = group * rows
    tile = min(512, keys)
    whole2 = lambda i: (0, 0)
    off = (offsets - lax.axis_index("key") * keys).reshape(1, rows)
    e, dp, qc, dl, st = pl.pallas_call(
        functools.partial(scores_kernel, scale, group, tile),
        grid=(heads // group,),
        in_specs=[
            vmem((group, rows, width), lambda i: (i, 0, 0)),
            vmem((group, rows, values), lambda i: (i, 0, 0)),
            vmem((group, nope, lat), lambda i: (i, 0, 0)),
            vmem((group, lat, values), lambda i: (i, 0, 0)),
            vmem((keys, full), whole2),
            vmem((1, rows), whole2),
        ],
        out_specs=[
            vmem((keys, span), lambda i: (0, i)),
            vmem((keys, span), lambda i: (0, i)),
            vmem((span, full), lambda i: (i, 0)),
            vmem((span, lat), lambda i: (i, 0)),
            vmem((3, heads, rows), lambda i: (0, 0, 0)),
        ],
        out_shape=[
            jax.ShapeDtypeStruct((keys, wide), bf16),
            jax.ShapeDtypeStruct((keys, wide), bf16),
            jax.ShapeDtypeStruct((wide, full), bf16),
            jax.ShapeDtypeStruct((wide, lat), bf16),
            jax.ShapeDtypeStruct((3, heads, rows), f32),
        ],
        scratch_shapes=[pltpu.VMEM((keys, span), f32)],
        compiler_params=pltpu.CompilerParams(vmem_limit_bytes=VMEM_BYTES),
    )(queries.transpose(1, 0, 2), out_grad.transpose(1, 0, 2), w_uk, w_uv, latent, off)
    joined = pl.pallas_call(
        functools.partial(stats_kernel, key_n),
        in_specs=[vmem()],
        out_specs=vmem(),
        out_shape=jax.ShapeDtypeStruct((2, heads, rows), f32),
        scratch_shapes=[
            pltpu.VMEM((key_n - 1, 3, heads, rows), f32),
            pltpu.SemaphoreType.DMA((key_n - 1,)),
            pltpu.SemaphoreType.DMA((key_n - 1,)),
        ],
        compiler_params=pltpu.CompilerParams(collective_id=0, has_side_effects=True),
    )(st)
    joined = joined.reshape(2, 1, wide)
    chunk = rows // key_n
    dlat, dq = pl.pallas_call(
        functools.partial(grads_kernel, scale, key_n, rows, min(512, wide)),
        grid=(keys // tile,),
        in_specs=[
            vmem((tile, wide), lambda i: (i, 0)),
            vmem((tile, wide), lambda i: (i, 0)),
            vmem((1, wide), whole2),
            vmem((1, wide), whole2),
            vmem((wide, full), whole2),
            vmem((wide, lat), whole2),
            vmem((full, tile), lambda i: (0, i)),
            vmem((heads, nope, lat), lambda i: (0, 0, 0)),
        ],
        out_specs=[
            vmem((tile, full), lambda i: (i, 0)),
            vmem((key_n, heads, chunk, width), lambda i: (0, 0, 0, 0)),
        ],
        out_shape=[
            jax.ShapeDtypeStruct((keys, full), bf16),
            jax.ShapeDtypeStruct((key_n, heads, chunk, width), bf16),
        ],
        scratch_shapes=[
            pltpu.VMEM((tile, wide), bf16),
            pltpu.VMEM((tile, wide), bf16),
            pltpu.VMEM((full, wide), f32),
        ],
        compiler_params=pltpu.CompilerParams(vmem_limit_bytes=VMEM_BYTES),
    )(e, dp, joined[0], joined[1], qc, dl, latent.T, w_uk)
    bits = head_n.bit_length() - 1
    d_latent, dq_sum = pl.pallas_call(
        functools.partial(joins_kernel, key_n, head_n),
        in_specs=[vmem(), vmem()],
        out_specs=[vmem(), vmem()],
        out_shape=[
            jax.ShapeDtypeStruct((keys, full), bf16),
            jax.ShapeDtypeStruct((heads, chunk, width), bf16),
        ],
        scratch_shapes=[
            pltpu.VMEM((keys, full), bf16),
            pltpu.VMEM((keys, full), bf16),
            pltpu.VMEM((key_n - 1, heads, chunk, width), bf16),
            pltpu.SemaphoreType.DMA((2, bits)),
            pltpu.SemaphoreType.DMA((2, bits)),
            pltpu.SemaphoreType.DMA((2, bits)),
            pltpu.SemaphoreType.DMA((2, bits)),
            pltpu.SemaphoreType.DMA((key_n - 1,)),
            pltpu.SemaphoreType.DMA((key_n - 1,)),
        ],
        compiler_params=pltpu.CompilerParams(
            vmem_limit_bytes=VMEM_BYTES, collective_id=1, has_side_effects=True
        ),
    )(dlat, dq)
    return (dq_sum.transpose(1, 0, 2), d_latent)


def solution(mesh):
    return jax.shard_map(
        functools.partial(shards, mesh.shape["key"], mesh.shape["head"]),
        mesh=mesh,
        in_specs=(
            P(None, "head", None),
            P("head", None, None),
            P("head", None, None),
            P("key", None),
            P(None, "head", None),
            P(),
        ),
        out_specs=(P("key", "head", None), P("key", None)),
        check_vma=False,
    )
```

time: 233 us -> 124 us (0.53)
  blocking collectives: 138 us -> 0 us
  Pallas kernels: 0 us -> 108 us
  matrix products: 53.9 us -> 0 us
  other arithmetic: 22.8 us -> 1.31 us
  between operations: 14.3 us -> 0.66 us
  local copies, waits for them, and re-layouts: 3.72 us -> 14.2 us
    psum x2 -> x0, blocking collectives: 110 us -> none  [the longest x1 98.2 us: shards(): lax.psum(jnp.concatenate([from_scores[:, :lat_width] + from_values, from_...]
    pallas_call x0 -> x4, Pallas kernels: none -> 108 us  [the longest x1 40.5 us: shards(): pl.pallas_call(functools.partial(joins_kernel, key_n, head_n), in_specs=[...]
    dot_general x8 -> x0, matrix products: 53.9 us -> none  [the longest x1 16.4 us: shards(): jnp.einsum('rhc,kc->hrk', d_lat, latent[:, :lat_width], preferred_element...]
    all_gather x2 -> x0, blocking collectives: 28.2 us -> none  [joined(): gathered = jax.tree.map(lambda a: lax.all_gather(a, axis), part)]
    convert_element_type x2 -> x0, other arithmetic: 14.9 us -> none  [the longest x1 13.1 us: shards(): d_scores = (probs * (d_probs - delta[..., None])).astype(jnp.bfloat16)]
    unnamed x24 -> x7, local copies, waits for them, and re-layouts: 0.51 us -> 12.9 us
    reduce_sum x1 -> x0, other arithmetic: 5.03 us -> none  [shards(): jnp.sum(jnp.where(visible, jnp.exp(masked - local_top[..., None]), 0.0),...]
    concatenate x2 -> x0, other arithmetic: 2.53 us -> none  [the longest x1 2.42 us: shards(): jnp.concatenate([from_scores[:, :lat_width] + from_values, from_scores[:,...]
  transfers between devices with their start and end apart: 1 -> 0, of which waited for: 0 -> 0; matrix products, arithmetic and copies ran while one was open for 8% -> 0% of each run, Pallas kernels for 0% -> 0%
where the time goes in v1:
time: 124 us
  Pallas kernels  108 us (87%)
  local copies, waits for them, and re-layouts  14.2 us (11%)
  other arithmetic  1.31 us (1%)
    pallas_call x1, Pallas kernels, shards(): pl.pallas_call(functools.partial(joins_kernel, key_n, head_n), in_specs=[...  40.5 us
    pallas_call x1, Pallas kernels, shards(): pl.pallas_call(functools.partial(grads_kernel, scale, key_n, rows, min(51...  33.9 us
    pallas_call x1, Pallas kernels, shards(): pl.pallas_call(functools.partial(scores_kernel, scale, group, tile), grid...  24.2 us
    unnamed x7, local copies, waits for them, and re-layouts  12.9 us
    pallas_call x1, Pallas kernels, shards(): pl.pallas_call(functools.partial(stats_kernel, key_n), in_specs=[vmem()],...  9.29 us

profile of v1, /device:TPU:0, one launch (start us, length us, event | category | flops | bytes accessed | tf_op | source)
XLA Modules:
  0.0 124.1 jit_solution(1391088422764678898)
XLA Ops:
  0.6 0.0 copy-start
  0.6 1.3 %subtract_bitcast_fusion.off_ref = s32[1,128]{1,0:T(1,128)} fusion(s32[128]{0:T(128)} %param.11, s32[]{:T(128)S(6)} %mul.3), kind=kLoop, calls=%fused_computation.1 | loop fusion | flops 128 | bytes 1028 | tf_op jit(solution)/shard_map/reshape | solution.py:260
  2.0 2.0 %copy.14 = bf16[128,16,128]{2,0,1:T(8,128)(2,1)} copy(bf16[128,16,128]{2,1,0:T(8,128)(2,1)} %param.10) | data formatting | bytes 1048576 | tf_op args[4]
  4.0 2.2 %copy.8 = bf16[128,16,192]{2,0,1:T(8,128)(2,1)} copy(bf16[128,16,192]{0,2,1:T(8,128)(2,1)} %param.6) | data formatting | bytes 1572864 | tf_op args[0]
  6.2 0.0 copy-done
  6.2 2.6 %copy.10.lat_ref = bf16[2048,576]{1,0:T(8,128)(2,1)} copy(bf16[2048,576]{0,1:T(8,128)(2,1)S(1)} %copy-done) | data formatting | bytes 4718592 | tf_op args[3]
  8.8 24.2 %shard_map.77 = (bf16[2048,2048]{1,0:T(8,128)(2,1)}, bf16[2048,2048]{1,0:T(8,128)(2,1)}, bf16[2048,576]{1,0:T(8,128)(2,1)}, bf16[2048,512]{1,0:T(8,128)(2,1)}, f32[3,16,128]{2,1,0:T(8,128)}) custom-call(bf16[16,128,192]{2,1,0:T(8,128)(2,1)} %bitcast.11, bf16[16,128,128]{2,1,0:T(8,128)(2,1)} %bitcast.12, bf16[16,128,512]{2,1,0:T(8,128)(2,1)} %uk_ref.3, ...), custom_call_target="tpu_custom_call" | custom-call | tf_op jit(solution)/shard_map/pallas_call | solution.py:261
  33.0 9.3 %shard_map.78 = f32[2,16,128]{2,1,0:T(8,128)} custom-call(f32[3,16,128]{2,1,0:T(8,128)} %get-tuple-element.13.st_ref), custom_call_target="tpu_custom_call" | custom-call | tf_op jit(solution)/shard_map/pallas_call | solution.py:289
  42.3 1.3 %fusion = (f32[1,16,128]{2,1,0:T(8,128)}, f32[1,16,128]{2,1,0:T(8,128)}) fusion(f32[2,16,128]{2,1,0:T(8,128)} %shard_map.78), kind=kLoop, calls=%fused_computation.2 | loop fusion | bytes 32768 | tf_op jit(solution)/shard_map/slice | solution.py:330
  43.6 33.9 %shard_map.79 = (bf16[2048,576]{1,0:T(8,128)(2,1)}, bf16[4,16,32,192]{3,2,1,0:T(8,128)(2,1)}) custom-call(bf16[2048,2048]{1,0:T(8,128)(2,1)} %get-tuple-element.11.e_ref, bf16[2048,2048]{1,0:T(8,128)(2,1)} %get-tuple-element.12.dp_ref, f32[1,2048]{1,0:T(1,128)} %bitcast.15, f32[1,2048]{1,0:T(1,128)} %bitcast.14, bf16[2048,576]{1,0:T(8,128)(2,1)} %get-tuple-element.14.qc_ref, ...), custom_call_target="tpu_custom_call" | custom-call | tf_op jit(solution)/shard_map/pallas_call | solution.py:303
  77.5 40.5 %shard_map.80 = (bf16[2048,576]{1,0:T(8,128)(2,1)}, bf16[16,32,192]{2,1,0:T(8,128)(2,1)}) custom-call(bf16[2048,576]{1,0:T(8,128)(2,1)} %get-tuple-element.16.dlat_ref, bf16[4,16,32,192]{3,2,1,0:T(8,128)(2,1)} %get-tuple-element.17.dq_ref), custom_call_target="tpu_custom_call" | custom-call | tf_op jit(solution)/shard_map/pallas_call | solution.py:332
  118.0 1.8 %copy.11 = bf16[32,16,192]{2,1,0:T(8,128)(2,1)} copy(bf16[32,16,192]{2,0,1:T(8,128)(2,1)} %bitcast.13) | data formatting | bytes 393216
  119.8 4.3 %copy.12 = bf16[2048,576]{0,1:T(8,128)(2,1)} copy(bf16[2048,576]{1,0:T(8,128)(2,1)} %get-tuple-element.21) | data formatting | bytes 4718592
Async XLA Ops:
  0.6 5.5 %copy-start = (bf16[2048,576]{0,1:T(8,128)(2,1)S(1)}, bf16[2048,576]{0,1:T(8,128)(2,1)}, u32[]{:S(2)}) copy-start(bf16[2048,576]{0,1:T(8,128)(2,1)} %param.9) | copy-start | bytes 7077892

commit v2 on v0

v2 whole, which is shorter than its diff:
```python
import functools
import math

import jax
import jax.numpy as jnp
from jax import lax
from jax.experimental import pallas as pl
from jax.experimental.pallas import tpu as pltpu
from jax.sharding import PartitionSpec as P

floor_score = -1e30
MESH = pl.DeviceIdType.MESH
f32 = jnp.float32
bf16 = jnp.bfloat16
VMEM_BYTES = 60 * 1024 * 1024
TILE = 512
BLOCK = 512


def dot(a, b):
    return lax.dot_general(a, b, (((1,), (0,)), ((), ())), preferred_element_type=f32)


def dot_t(a, b):
    return lax.dot_general(a, b, (((1,), (1,)), ((), ())), preferred_element_type=f32)


def dot_c(a, b):
    return lax.dot_general(a, b, (((0,), (0,)), ((), ())), preferred_element_type=f32)


def scores_kernel(
    scale, group, tile, q_ref, og_ref, uk_ref, uv_ref, lt_ref, off_ref,
    e_ref, dp_ref, qc_ref, dl_ref, st_ref, tops_ref, lat_ref,
):
    step = pl.program_id(0)
    rows = q_ref.shape[2]
    nope = uk_ref.shape[1]
    width = uk_ref.shape[2]
    keys = lt_ref.shape[1]

    @pl.when(step == 0)
    def _():
        lat_ref[...] = lt_ref[...].T

    for h in range(group):
        cut = slice(h * rows, (h + 1) * rows)
        qc_ref[:width, cut] = dot_c(uk_ref[h], q_ref[h, :nope, :]).astype(bf16)
        qc_ref[width:, cut] = q_ref[h, nope:, :]
        dl_ref[:, cut] = dot_t(uv_ref[h], og_ref[h]).astype(bf16)
    qc = qc_ref[...]
    dl = dl_ref[...]
    off = jnp.concatenate([off_ref[...]] * group, axis=1)
    tops = []
    totals = []
    accs = []
    for t in range(keys // tile):
        at = pl.ds(t * tile, tile)
        s = dot(lat_ref[at, :], qc) * scale
        dp = dot(lat_ref[at, :width], dl).astype(bf16)
        position = lax.broadcasted_iota(jnp.int32, s.shape, 0)
        s = jnp.where(position <= off - t * tile, s, floor_score)
        top = jnp.maximum(jnp.max(s, axis=0, keepdims=True), 0.5 * floor_score)
        e = jnp.exp(s - top).astype(bf16)
        e_ref[at, :] = e
        dp_ref[at, :] = dp
        e = e.astype(f32)
        tops.append(top)
        totals.append(jnp.sum(e, axis=0, keepdims=True))
        accs.append(jnp.sum(e * dp.astype(f32), axis=0, keepdims=True))
    best = functools.reduce(jnp.maximum, tops)
    total = 0.0
    acc = 0.0
    for top, a, b in zip(tops, totals, accs):
        near = jnp.exp(top - best)
        total = total + near * a
        acc = acc + near * b
    for h in range(group):
        cut = slice(h * rows, (h + 1) * rows)
        at = pl.ds(step * group + h, 1)
        st_ref[0, at, :] = best[:, cut]
        st_ref[1, at, :] = total[:, cut]
        st_ref[2, at, :] = acc[:, cut]
        for t, top in enumerate(tops):
            tops_ref[t, at, :] = top[:, cut]


def grads_kernel(
    scale, key_n, head_n, rows, tile, block, group,
    e_hbm, dp_hbm, qc_hbm, dl_hbm, lt_hbm, uk_hbm, st_ref, tops_ref,
    out_ref, dqo_ref,
    e_ref, dp_ref, qc_ref, dl_ref, lt_ref, uk_ref, norm_ref, delta_ref, part_ref, got_ref,
    dq_ref, dqg_ref, stg_ref,
    e_sem, dp_sem, in_sem, st_send, st_recv, rs_send, rs_recv, ag_send, ag_recv, q_send, q_recv,
):
    mk = lax.axis_index("key")
    mh = lax.axis_index("head")
    bits = head_n.bit_length() - 1
    keys = e_ref.shape[0]
    wide = e_ref.shape[1]
    width = dl_ref.shape[0]
    nope = uk_ref.shape[1]
    full = qc_ref.shape[0]
    blocks = keys // block
    span = group * rows
    groups = wide // span
    piece = full // head_n
    chunk = rows // key_n

    def bit(b):
        return lax.rem(lax.div(mh, 1 << b), 2)

    def partner(b):
        return mh + (1 - 2 * bit(b)) * (1 << b)

    barrier = pltpu.get_barrier_semaphore()
    for d in range(1, key_n):
        pl.semaphore_signal(
            barrier, inc=1, device_id={"key": lax.rem(mk + d, key_n)}, device_id_type=MESH
        )
    for b in range(bits):
        pl.semaphore_signal(
            barrier, inc=1, device_id={"head": partner(b)}, device_id_type=MESH
        )

    def local(a, b, sem):
        copy = pltpu.make_async_copy(a, b, sem)
        copy.start()
        return copy

    e_in = []
    dp_in = []
    weights = []
    for b in range(blocks):
        at = pl.ds(b * block, block)
        e_in.append(local(e_hbm.at[at], e_ref.at[at], e_sem.at[b]))
        dp_in.append(local(dp_hbm.at[at], dp_ref.at[at], dp_sem.at[b]))
        if b == 0:
            weights.append(local(qc_hbm, qc_ref, in_sem.at[0]))
            weights.append(local(dl_hbm, dl_ref, in_sem.at[1]))
    weights.append(local(lt_hbm, lt_ref, in_sem.at[2]))
    weights.append(local(uk_hbm, uk_ref, in_sem.at[3]))

    pl.semaphore_wait(barrier, key_n - 1 + bits)

    def remote(src, dst, send, recv, where):
        copy = pltpu.make_async_remote_copy(
            src_ref=src, dst_ref=dst, send_sem=send, recv_sem=recv,
            device_id=where, device_id_type=MESH,
        )
        copy.start()
        return copy

    copies = []
    for d in range(1, key_n):
        copies.append(
            remote(
                st_ref, stg_ref.at[d - 1], st_send.at[d - 1], st_recv.at[d - 1],
                {"key": lax.rem(mk + d, key_n)},
            )
        )
    for copy in copies:
        copy.wait()
    best = st_ref[0]
    for d in range(key_n - 1):
        best = jnp.maximum(best, stg_ref[d, 0])
    near = jnp.exp(st_ref[0] - best)
    total = near * st_ref[1]
    acc = near * st_ref[2]
    for d in range(key_n - 1):
        near = jnp.exp(stg_ref[d, 0] - best)
        total = total + near * stg_ref[d, 1]
        acc = acc + near * stg_ref[d, 2]
    delta_ref[...] = acc / total
    for t in range(keys // tile):
        norm_ref[t] = jnp.exp(tops_ref[t] - best) / total

    def row(ref, g, t=None):
        pick = (lambda i: ref[pl.ds(i, 1), :]) if t is None else (lambda i: ref[t, pl.ds(i, 1), :])
        return jnp.concatenate([pick(g * group + h) for h in range(group)], axis=1)

    def latent_block(b):
        e_in[b].wait()
        dp_in[b].wait()
        if b == 0:
            weights[0].wait()
            weights[1].wait()
        at = pl.ds(b * block, block)
        for g in range(groups):
            cut = slice(g * span, (g + 1) * span)
            p = e_ref[at, cut].astype(f32) * row(norm_ref, g, b * block // tile)
            e_ref[at, cut] = p.astype(bf16)
            dp_ref[at, cut] = (p * (dp_ref[at, cut].astype(f32) - row(delta_ref, g))).astype(bf16)
        from_scores = dot_t(qc_ref[...], dp_ref[at, :]) * scale
        from_values = dot_t(dl_ref[...], e_ref[at, :])
        summed = jnp.concatenate(
            [from_scores[:width] + from_values, from_scores[width:]], axis=0
        )
        for j in range(head_n):
            part_ref[b, j] = summed[j * piece : (j + 1) * piece].astype(bf16)

    q_copies = []

    def query_group(g):
        if g == 0:
            weights[2].wait()
            weights[3].wait()
        cut = slice(g * span, (g + 1) * span)
        dq = dot(lt_ref[...], dp_ref[:, cut]) * scale
        high = dq[:width].astype(bf16)
        low = (dq[:width] - high.astype(f32)).astype(bf16)
        for h in range(group):
            mine = slice(h * rows, (h + 1) * rows)
            w = uk_ref[g * group + h]
            a = (dot(w, high[:, mine]) + dot(w, low[:, mine])).T
            r = dq[width:, mine].T
            for j in range(key_n):
                at = slice(j * chunk, (j + 1) * chunk)
                dq_ref[j, g, h, :, :nope] = a[at].astype(bf16)
                dq_ref[j, g, h, :, nope:] = r[at].astype(bf16)
        for d in range(1, key_n):
            to = lax.rem(mk + d, key_n)
            q_copies.append(
                remote(
                    dq_ref.at[to, g], dqg_ref.at[d - 1, g],
                    q_send.at[d - 1, g], q_recv.at[d - 1, g], {"key": to},
                )
            )

    orders = [[0] + list(range(1, bits)), [0] + list(range(bits - 1, 0, -1))]
    flight = [None] * blocks
    base = [0] * blocks
    stage = [0] * blocks

    def advance(b):
        k = stage[b]
        order = orders[b % 2]
        if k > 0:
            flight[b].wait()
        if 0 < k <= bits:
            size = head_n >> k
            spot = head_n - (head_n >> (k - 1))
            for j in range(size):
                summed = part_ref[b, base[b] + j].astype(f32) + got_ref[b, spot + j].astype(f32)
                if k == bits:
                    out_ref[b, base[b] + j] = summed.astype(bf16)
                else:
                    part_ref[b, base[b] + j] = summed.astype(bf16)
        if k < bits:
            size = head_n >> (k + 1)
            spot = head_n - (head_n >> k)
            v = bit(order[k])
            flight[b] = remote(
                part_ref.at[b, pl.ds(base[b] + (1 - v) * size, size)],
                got_ref.at[b, pl.ds(spot, size)],
                rs_send.at[b, k], rs_recv.at[b, k], {"head": partner(order[k])},
            )
            base[b] = base[b] + v * size
        elif k < 2 * bits:
            i = k - bits
            size = 1 << i
            if i > 0:
                base[b] = base[b] - bit(order[bits - i]) * (size // 2)
            at = pl.ds(base[b], size)
            flight[b] = remote(
                out_ref.at[b, at], out_ref.at[b, at],
                ag_send.at[b, i], ag_recv.at[b, i], {"head": partner(order[bits - 1 - i])},
            )
        stage[b] = k + 1

    def sweep(last):
        for b in range(last):
            if stage[b] <= 2 * bits:
                advance(b)

    for b in range(blocks):
        latent_block(b)
        sweep(b + 1)
    for g in range(groups):
        query_group(g)
        sweep(blocks)
    while min(stage) <= 2 * bits:
        sweep(blocks)
    for copy in q_copies:
        copy.wait()
    for g in range(groups):
        summed = dq_ref[mk, g].astype(f32)
        for d in range(key_n - 1):
            summed = summed + dqg_ref[d, g].astype(f32)
        dqo_ref[g] = summed.astype(bf16)


def vmem(shape=None, index=None):
    return pl.BlockSpec(shape, index, memory_space=pltpu.VMEM)


def shards(key_n, head_n, queries, w_uk, w_uv, latent, out_grad, offsets):
    rows, heads, width = queries.shape
    keys, full = latent.shape
    nope = w_uk.shape[1]
    lat = w_uk.shape[2]
    values = out_grad.shape[2]
    scale = 1.0 / math.sqrt(width)
    wide = heads * rows
    group = 4 if heads % 4 == 0 else heads
    groups = heads // group
    span = group * rows
    tile = min(TILE, keys)
    tiles = keys // tile
    block = min(BLOCK, keys)
    blocks = keys // block
    off = (offsets - lax.axis_index("key") * keys).reshape(1, rows)
    flipped = latent.T
    e, dp, qc, dl, st, tops = pl.pallas_call(
        functools.partial(scores_kernel, scale, group, tile),
        grid=(groups,),
        in_specs=[
            vmem((group, width, rows), lambda i: (i, 0, 0)),
            vmem((group, rows, values), lambda i: (i, 0, 0)),
            vmem((group, nope, lat), lambda i: (i, 0, 0)),
            vmem((group, lat, values), lambda i: (i, 0, 0)),
            vmem((full, keys), lambda i: (0, 0)),
            vmem((1, rows), lambda i: (0, 0)),
        ],
        out_specs=[
            vmem((keys, span), lambda i: (0, i)),
            vmem((keys, span), lambda i: (0, i)),
            vmem((full, span), lambda i: (0, i)),
            vmem((lat, span), lambda i: (0, i)),
            vmem((3, heads, rows), lambda i: (0, 0, 0)),
            vmem((tiles, heads, rows), lambda i: (0, 0, 0)),
        ],
        out_shape=[
            jax.ShapeDtypeStruct((keys, wide), bf16),
            jax.ShapeDtypeStruct((keys, wide), bf16),
            jax.ShapeDtypeStruct((full, wide), bf16),
            jax.ShapeDtypeStruct((lat, wide), bf16),
            jax.ShapeDtypeStruct((3, heads, rows), f32),
            jax.ShapeDtypeStruct((tiles, heads, rows), f32),
        ],
        scratch_shapes=[pltpu.VMEM((keys, full), bf16)],
        compiler_params=pltpu.CompilerParams(vmem_limit_bytes=VMEM_BYTES),
    )(queries.transpose(1, 2, 0), out_grad.transpose(1, 0, 2), w_uk, w_uv, flipped, off)
    bits = head_n.bit_length() - 1
    chunk = rows // key_n
    piece = full // head_n
    dma = pltpu.SemaphoreType.DMA
    anywhere = pl.BlockSpec(memory_space=pl.ANY)
    d_latent, dq = pl.pallas_call(
        functools.partial(grads_kernel, scale, key_n, head_n, rows, tile, block, group),
        in_specs=[anywhere] * 6 + [vmem(), vmem()],
        out_specs=[vmem(), vmem()],
        out_shape=[
            jax.ShapeDtypeStruct((blocks, head_n, piece, block), bf16),
            jax.ShapeDtypeStruct((groups, group, chunk, width), bf16),
        ],
        scratch_shapes=[
            pltpu.VMEM((keys, wide), bf16),
            pltpu.VMEM((keys, wide), bf16),
            pltpu.VMEM((full, wide), bf16),
            pltpu.VMEM((lat, wide), bf16),
            pltpu.VMEM((full, keys), bf16),
            pltpu.VMEM((heads, nope, lat), bf16),
            pltpu.VMEM((tiles, heads, rows), f32),
            pltpu.VMEM((heads, rows), f32),
            pltpu.VMEM((blocks, head_n, piece, block), bf16),
            pltpu.VMEM((blocks, head_n, piece, block), bf16),
            pltpu.VMEM((key_n, groups, group, chunk, width), bf16),
            pltpu.VMEM((key_n - 1, groups, group, chunk, width), bf16),
            pltpu.VMEM((key_n - 1, 3, heads, rows), f32),
            dma((blocks,)),
            dma((blocks,)),
            dma((4,)),
            dma((key_n - 1,)),
            dma((key_n - 1,)),
            dma((blocks, bits)),
            dma((blocks, bits)),
            dma((blocks, bits)),
            dma((blocks, bits)),
            dma((key_n - 1, groups)),
            dma((key_n - 1, groups)),
        ],
        compiler_params=pltpu.CompilerParams(
            vmem_limit_bytes=VMEM_BYTES, collective_id=0, has_side_effects=True
        ),
    )(e, dp, qc, dl, flipped, w_uk, st, tops)
    d_latent = d_latent.transpose(1, 2, 0, 3).reshape(full, keys).T
    return (dq.reshape(heads, chunk, width).transpose(1, 0, 2), d_latent)


def solution(mesh):
    return jax.shard_map(
        functools.partial(shards, mesh.shape["key"], mesh.shape["head"]),
        mesh=mesh,
        in_specs=(
            P(None, "head", None),
            P("head", None, None),
            P("head", None, None),
            P("key", None),
            P(None, "head", None),
            P(),
        ),
        out_specs=(P("key", "head", None), P("key", None)),
        check_vma=False,
    )
```

time: 233 us -> 85 us (0.36)
  blocking collectives: 138 us -> 0 us
  Pallas kernels: 0 us -> 73.5 us
  matrix products: 53.9 us -> 0 us
  other arithmetic: 22.8 us -> 1.18 us
  between operations: 14.3 us -> 0.65 us
  local copies, waits for them, and re-layouts: 3.72 us -> 9.38 us
    psum x2 -> x0, blocking collectives: 110 us -> none  [the longest x1 98.2 us: shards(): lax.psum(jnp.concatenate([from_scores[:, :lat_width] + from_values, from_...]
    pallas_call x0 -> x2, Pallas kernels: none -> 73.5 us  [the longest x1 51.8 us: shards(): pl.pallas_call(functools.partial(grads_kernel, scale, key_n, head_n, rows...]
    dot_general x8 -> x0, matrix products: 53.9 us -> none  [the longest x1 16.4 us: shards(): jnp.einsum('rhc,kc->hrk', d_lat, latent[:, :lat_width], preferred_element...]
    all_gather x2 -> x0, blocking collectives: 28.2 us -> none  [joined(): gathered = jax.tree.map(lambda a: lax.all_gather(a, axis), part)]
    convert_element_type x2 -> x0, other arithmetic: 14.9 us -> none  [the longest x1 13.1 us: shards(): d_scores = (probs * (d_probs - delta[..., None])).astype(jnp.bfloat16)]
    reduce_sum x1 -> x0, other arithmetic: 5.03 us -> none  [shards(): jnp.sum(jnp.where(visible, jnp.exp(masked - local_top[..., None]), 0.0),...]
    unnamed x24 -> x2, local copies, waits for them, and re-layouts: 0.51 us -> 4.09 us
    transpose x0 -> x1, local copies, waits for them, and re-layouts: none -> 3.49 us  [shards(): d_latent = d_latent.transpose(1, 2, 0, 3).reshape(full, keys).T]
  transfers between devices with their start and end apart: 1 -> 0, of which waited for: 0 -> 0; matrix products, arithmetic and copies ran while one was open for 8% -> 0% of each run, Pallas kernels for 0% -> 0%
where the time goes in v2:
time: 85 us; the launch traced here: 84.7 us
  Pallas kernels  73.5 us (86%)
  local copies, waits for them, and re-layouts  9.38 us (11%)
  other arithmetic  1.18 us (1%)
    pallas_call x1, Pallas kernels, shards(): pl.pallas_call(functools.partial(grads_kernel, scale, key_n, head_n, rows...  51.8 us
    pallas_call x1, Pallas kernels, shards(): pl.pallas_call(functools.partial(scores_kernel, scale, group, tile), grid...  21.7 us
    unnamed x2, local copies, waits for them, and re-layouts  4.09 us
    transpose x1, local copies, waits for them, and re-layouts, shards(): d_latent = d_latent.transpose(1, 2, 0, 3).reshape(full, keys).T  3.49 us
    reshape x1, local copies, waits for them, and re-layouts, shards(): return (dq.reshape(heads, chunk, width).transpose(1, 0, 2), d_latent)  1.8 us

profile of v2, /device:TPU:0, one launch (start us, length us, event | category | flops | bytes accessed | tf_op | source)
XLA Modules:
  0.0 84.7 jit_solution(2025669334366451520)
XLA Ops:
  0.6 1.2 %subtract_bitcast_fusion.off_ref = s32[1,128]{1,0:T(1,128)} fusion(s32[128]{0:T(128)} %param.11, s32[]{:T(128)S(6)} %mul.3), kind=kLoop, calls=%fused_computation.2 | loop fusion | flops 128 | bytes 1028 | tf_op jit(solution)/shard_map/reshape | solution.py:312
  1.8 2.0 %copy.16 = bf16[128,16,128]{2,0,1:T(8,128)(2,1)} copy(bf16[128,16,128]{2,1,0:T(8,128)(2,1)} %param.10) | data formatting | bytes 1048576 | tf_op args[4]
  3.8 21.7 %shard_map.77 = (bf16[2048,2048]{1,0:T(8,128)(2,1)}, bf16[2048,2048]{1,0:T(8,128)(2,1)}, bf16[576,2048]{1,0:T(8,128)(2,1)}, bf16[512,2048]{1,0:T(8,128)(2,1)}, f...) custom-call(bf16[16,192,128]{2,1,0:T(8,128)(2,1)} %bitcast.23, bf16[16,128,128]{2,1,0:T(8,128)(2,1)} %bitcast.22, ...), custom_call_target="tpu_custom_call" | custom-call | tf_op jit(solution)/shard_map/pallas_call | solution.py:314
  25.4 51.8 %shard_map.78 = (bf16[4,8,72,512]{3,2,1,0:T(8,128)(2,1)}, bf16[4,4,32,192]{3,2,1,0:T(8,128)(2,1)}) custom-call(bf16[2048,2048]{1,0:T(8,128)(2,1)} %get-tuple-element.10.e_hbm, bf16[2048,2048]{1,0:T(8,128)(2,1)} %get-tuple-element.11.dp_hbm, bf16[576,2048]{1,0:T(8,128)(2,1)} %get-tuple-element.12.qc_hbm, bf16[512,2048]{1,0:T(8,128)(2,1)} %get-tuple-element.13.dl_hbm, ...), custom_call_target="tpu_custom_call" | custom-call | tf_op jit(solution)/shard_map/pallas_call | solution.py:349
  77.3 1.8 %copy.17 = bf16[16,32,192]{2,0,1:T(8,128)(2,1)} copy(bf16[16,32,192]{2,1,0:T(8,128)(2,1)} %bitcast.25) | data formatting | bytes 393216 | tf_op jit(solution)/shard_map/reshape | solution.py:388
  79.1 3.5 %copy.12 = bf16[8,72,4,512]{3,2,1,0:T(4,128)(2,1)S(1)} copy(bf16[8,72,4,512]{3,1,0,2:T(8,128)(2,1)} %bitcast.20) | data formatting | bytes 4718592 | tf_op jit(solution)/shard_map/transpose | solution.py:387
  82.6 2.1 %copy.13 = bf16[72,8,4,512]{3,1,2,0:T(8,128)(2,1)} copy(bf16[72,8,4,512]{3,2,1,0:T(4,128)(2,1)S(1)} %bitcast.17) | data formatting | bytes 4718592

commit v3 on v2

--- a/solution.py
+++ b/solution.py
@@ -23,6 +23,7 @@
 
 def dot_t(a, b):
     return lax.dot_general(a, b, (((1,), (1,)), ((), ())), preferred_element_type=f32)
+LONG = (2, 5)
 
 
 def dot_c(a, b):
@@ -50,29 +51,30 @@
         dl_ref[:, cut] = dot_t(uv_ref[h], og_ref[h]).astype(bf16)
     qc = qc_ref[...]
     dl = dl_ref[...]
-    off = jnp.concatenate([off_ref[...]] * group, axis=1)
+    unit = scale * math.log2(math.e)
+    off = jnp.concatenate([off_ref[...] - lax.axis_index("key") * keys] * group, axis=1)
     tops = []
     totals = []
     accs = []
     for t in range(keys // tile):
         at = pl.ds(t * tile, tile)
-        s = dot(lat_ref[at, :], qc) * scale
+        s = dot(lat_ref[at, :], qc)
         dp = dot(lat_ref[at, :width], dl).astype(bf16)
         position = lax.broadcasted_iota(jnp.int32, s.shape, 0)
         s = jnp.where(position <= off - t * tile, s, floor_score)
         top = jnp.maximum(jnp.max(s, axis=0, keepdims=True), 0.5 * floor_score)
-        e = jnp.exp(s - top).astype(bf16)
+        e = jnp.exp2((s - top) * unit).astype(bf16)
         e_ref[at, :] = e
         dp_ref[at, :] = dp
         e = e.astype(f32)
-        tops.append(top)
+        tops.append(top * unit)
         totals.append(jnp.sum(e, axis=0, keepdims=True))
         accs.append(jnp.sum(e * dp.astype(f32), axis=0, keepdims=True))
     best = functools.reduce(jnp.maximum, tops)
     total = 0.0
     acc = 0.0
     for top, a, b in zip(tops, totals, accs):
-        near = jnp.exp(top - best)
+        near = jnp.exp2(top - best)
         total = total + near * a
         acc = acc + near * b
     for h in range(group):
@@ -106,6 +108,8 @@
     groups = wide // span
     piece = full // head_n
     chunk = rows // key_n
+    rotary = full - width
+    pair = nope // rotary
 
     def bit(b):
         return lax.rem(lax.div(mh, 1 << b), 2)
@@ -164,33 +168,38 @@
     best = st_ref[0]
     for d in range(key_n - 1):
         best = jnp.maximum(best, stg_ref[d, 0])
-    near = jnp.exp(st_ref[0] - best)
+    near = jnp.exp2(st_ref[0] - best)
     total = near * st_ref[1]
     acc = near * st_ref[2]
     for d in range(key_n - 1):
-        near = jnp.exp(stg_ref[d, 0] - best)
+        near = jnp.exp2(stg_ref[d, 0] - best)
         total = total + near * stg_ref[d, 1]
         acc = acc + near * stg_ref[d, 2]
     delta_ref[...] = acc / total
     for t in range(keys // tile):
-        norm_ref[t] = jnp.exp(tops_ref[t] - best) / total
+        norm_ref[t] = jnp.exp2(tops_ref[t] - best) / total
 
     def row(ref, g, t=None):
         pick = (lambda i: ref[pl.ds(i, 1), :]) if t is None else (lambda i: ref[t, pl.ds(i, 1), :])
         return jnp.concatenate([pick(g * group + h) for h in range(group)], axis=1)
 
-    def latent_block(b):
+    def prepare(b):
         e_in[b].wait()
         dp_in[b].wait()
-        if b == 0:
-            weights[0].wait()
-            weights[1].wait()
         at = pl.ds(b * block, block)
         for g in range(groups):
             cut = slice(g * span, (g + 1) * span)
             p = e_ref[at, cut].astype(f32) * row(norm_ref, g, b * block // tile)
             e_ref[at, cut] = p.astype(bf16)
             dp_ref[at, cut] = (p * (dp_ref[at, cut].astype(f32) - row(delta_ref, g))).astype(bf16)
+
+    def latent_block(b):
+        if b == 0:
+            weights[0].wait()
+            weights[1].wait()
+        if b + 1 < blocks:
+            prepare(b + 1)
+        at = pl.ds(b * block, block)
         from_scores = dot_t(qc_ref[...], dp_ref[at, :]) * scale
         from_values = dot_t(dl_ref[...], e_ref[at, :])
         summed = jnp.concatenate(
@@ -213,11 +222,13 @@
             mine = slice(h * rows, (h + 1) * rows)
             w = uk_ref[g * group + h]
             a = (dot(w, high[:, mine]) + dot(w, low[:, mine])).T
-            r = dq[width:, mine].T
             for j in range(key_n):
-                at = slice(j * chunk, (j + 1) * chunk)
-                dq_ref[j, g, h, :, :nope] = a[at].astype(bf16)
-                dq_ref[j, g, h, :, nope:] = r[at].astype(bf16)
+                dq_ref[j, g, h] = a[j * chunk : (j + 1) * chunk].astype(bf16)
+        for i in range(group // pair):
+            mine = [slice(h * rows, (h + 1) * rows) for h in range(i * pair, (i + 1) * pair)]
+            a = jnp.concatenate([dq[width:, m] for m in mine], axis=0).T
+            for j in range(key_n):
+                dq_ref[j, g, group + i] = a[j * chunk : (j + 1) * chunk].astype(bf16)
         for d in range(1, key_n):
             to = lax.rem(mk + d, key_n)
             q_copies.append(
@@ -243,7 +254,7 @@
             for j in range(size):
                 summed = part_ref[b, base[b] + j].astype(f32) + got_ref[b, spot + j].astype(f32)
                 if k == bits:
-                    out_ref[b, base[b] + j] = summed.astype(bf16)
+                    out_ref[base[b] + j, :, b * block : (b + 1) * block] = summed.astype(bf16)
                 else:
                     part_ref[b, base[b] + j] = summed.astype(bf16)
         if k < bits:
@@ -261,33 +272,46 @@
             size = 1 << i
             if i > 0:
                 base[b] = base[b] - bit(order[bits - i]) * (size // 2)
-            at = pl.ds(base[b], size)
+            at = out_ref.at[pl.ds(base[b], size), :, pl.ds(b * block, block)]
             flight[b] = remote(
-                out_ref.at[b, at], out_ref.at[b, at],
+                at, at,
                 ag_send.at[b, i], ag_recv.at[b, i], {"head": partner(order[bits - 1 - i])},
             )
         stage[b] = k + 1
 
-    def sweep(last):
-        for b in range(last):
-            if stage[b] <= 2 * bits:
-                advance(b)
-
-    for b in range(blocks):
-        latent_block(b)
-        sweep(b + 1)
-    for g in range(groups):
-        query_group(g)
-        sweep(blocks)
+    age = [0] * blocks
+    ready = [False] * blocks
+
+    def sweep(drain):
+        for b in range(blocks):
+            if ready[b] and stage[b] <= 2 * bits:
+                age[b] += 1
+                if drain or age[b] > (stage[b] in LONG):
+                    advance(b)
+                    age[b] = 0
+
+    work = [(latent_block, b) for b in range(blocks)]
+    work = work[:-1] + [(query_group, 0)] + work[-1:]
+    work += [(query_group, g) for g in range(1, groups)]
+    prepare(0)
+    for do, i in work:
+        do(i)
+        if do is latent_block:
+            ready[i] = True
+        sweep(False)
     while min(stage) <= 2 * bits:
-        sweep(blocks)
+        sweep(True)
     for copy in q_copies:
         copy.wait()
     for g in range(groups):
         summed = dq_ref[mk, g].astype(f32)
         for d in range(key_n - 1):
             summed = summed + dqg_ref[d, g].astype(f32)
-        dqo_ref[g] = summed.astype(bf16)
+        summed = summed.astype(bf16)
+        for h in range(group):
+            dqo_ref[g, h, :, :nope] = summed[h]
+            cut = slice(h % pair * rotary, (h % pair + 1) * rotary)
+            dqo_ref[g, h, :, nope:] = summed[group + h // pair][:, cut]
 
 
 def vmem(shape=None, index=None):
@@ -309,7 +333,7 @@
     tiles = keys // tile
     block = min(BLOCK, keys)
     blocks = keys // block
-    off = (offsets - lax.axis_index("key") * keys).reshape(1, rows)
+    off = offsets.reshape(1, rows)
     flipped = latent.T
     e, dp, qc, dl, st, tops = pl.pallas_call(
         functools.partial(scores_kernel, scale, group, tile),
@@ -344,6 +368,7 @@
     bits = head_n.bit_length() - 1
     chunk = rows // key_n
     piece = full // head_n
+    slots = group + group * (full - lat) // nope
     dma = pltpu.SemaphoreType.DMA
     anywhere = pl.BlockSpec(memory_space=pl.ANY)
     d_latent, dq = pl.pallas_call(
@@ -351,7 +376,7 @@
         in_specs=[anywhere] * 6 + [vmem(), vmem()],
         out_specs=[vmem(), vmem()],
         out_shape=[
-            jax.ShapeDtypeStruct((blocks, head_n, piece, block), bf16),
+            jax.ShapeDtypeStruct((head_n, piece, keys), bf16),
             jax.ShapeDtypeStruct((groups, group, chunk, width), bf16),
         ],
         scratch_shapes=[
@@ -365,8 +390,8 @@
             pltpu.VMEM((heads, rows), f32),
             pltpu.VMEM((blocks, head_n, piece, block), bf16),
             pltpu.VMEM((blocks, head_n, piece, block), bf16),
-            pltpu.VMEM((key_n, groups, group, chunk, width), bf16),
-            pltpu.VMEM((key_n - 1, groups, group, chunk, width), bf16),
+            pltpu.VMEM((key_n, groups, slots, chunk, nope), bf16),
+            pltpu.VMEM((key_n - 1, groups, slots, chunk, nope), bf16),
             pltpu.VMEM((key_n - 1, 3, heads, rows), f32),
             dma((blocks,)),
             dma((blocks,)),
@@ -384,7 +409,7 @@
             vmem_limit_bytes=VMEM_BYTES, collective_id=0, has_side_effects=True
         ),
     )(e, dp, qc, dl, flipped, w_uk, st, tops)
-    d_latent = d_latent.transpose(1, 2, 0, 3).reshape(full, keys).T
+    d_latent = d_latent.reshape(full, keys).T
     return (dq.reshape(heads, chunk, width).transpose(1, 0, 2), d_latent)
 
 

time: 85 us -> 88.1 us (1.036)
  Pallas kernels: 73.5 us -> 80 us
  local copies, waits for them, and re-layouts: 9.38 us -> 7.12 us
  other arithmetic: 1.18 us -> 0 us
    pallas_call x1, Pallas kernels: 51.8 us -> 59 us  [shards(): pl.pallas_call(functools.partial(grads_kernel, scale, key_n, head_n, rows...]
    transpose x1 -> x0, local copies, waits for them, and re-layouts: 3.49 us -> none  [shards(): d_latent = d_latent.transpose(1, 2, 0, 3).reshape(full, keys).T]
    unnamed x2, local copies, waits for them, and re-layouts: 4.09 us -> 5.32 us
    reshape x1 -> x0, other arithmetic: 1.18 us -> none  [shards(): off = (offsets - lax.axis_index('key') * keys).reshape(1, rows)]
where the time goes in v3:
time: 88.1 us; the launch traced here: 87.8 us
  Pallas kernels  80 us (91%)
  local copies, waits for them, and re-layouts  7.12 us (8%)
    pallas_call x1, Pallas kernels, shards(): pl.pallas_call(functools.partial(grads_kernel, scale, key_n, head_n, rows...  59 us
    pallas_call x1, Pallas kernels, shards(): pl.pallas_call(functools.partial(scores_kernel, scale, group, tile), grid...  21 us
    unnamed x2, local copies, waits for them, and re-layouts  5.32 us
    reshape x1, local copies, waits for them, and re-layouts, shards(): return (dq.reshape(heads, chunk, width).transpose(1, 0, 2), d_latent)  1.8 us

profile of v3, /device:TPU:0, one launch (start us, length us, event | category | flops | bytes accessed | tf_op | source)
XLA Modules:
  0.0 87.8 jit_solution(2081945351426568805)
XLA Ops:
  0.6 2.0 %copy.12 = bf16[128,16,128]{2,0,1:T(8,128)(2,1)} copy(bf16[128,16,128]{2,1,0:T(8,128)(2,1)} %param.10) | data formatting | bytes 1048576 | tf_op args[4]
  2.6 21.0 %shard_map.77 = (bf16[2048,2048]{1,0:T(8,128)(2,1)}, bf16[2048,2048]{1,0:T(8,128)(2,1)}, bf16[576,2048]{1,0:T(8,128)(2,1)}, bf16[512,2048]{1,0:T(8,128)(2,1)}, f...) custom-call(bf16[16,192,128]{2,1,0:T(8,128)(2,1)} %bitcast.17, bf16[16,128,128]{2,1,0:T(8,128)(2,1)} %bitcast.16, ...), custom_call_target="tpu_custom_call" | custom-call | tf_op jit(solution)/shard_map/pallas_call | solution.py:338
  23.6 59.0 %shard_map.78 = (bf16[8,72,2048]{2,1,0:T(8,128)(2,1)}, bf16[4,4,32,192]{3,2,1,0:T(8,128)(2,1)}) custom-call(bf16[2048,2048]{1,0:T(8,128)(2,1)} %get-tuple-element.10.e_hbm, bf16[2048,2048]{1,0:T(8,128)(2,1)} %get-tuple-element.11.dp_hbm, bf16[576,2048]{1,0:T(8,128)(2,1)} %get-tuple-element.12.qc_hbm, bf16[512,2048]{1,0:T(8,128)(2,1)} %get-tuple-element.13.dl_hbm, ...), custom_call_target="tpu_custom_call" | custom-call | tf_op jit(solution)/shard_map/pallas_call | solution.py:374
  82.6 1.8 %copy.13 = bf16[16,32,192]{2,0,1:T(8,128)(2,1)} copy(bf16[16,32,192]{2,1,0:T(8,128)(2,1)} %bitcast.19) | data formatting | bytes 393216 | tf_op jit(solution)/shard_map/reshape | solution.py:413
  84.4 3.4 %copy.15 = bf16[2048,576]{0,1:T(8,128)(2,1)} copy(bf16[2048,576]{0,1:T(8,128)(2,1)} %bitcast.15) | data formatting | bytes 4718592

commit v4 on v3

--- a/solution.py
+++ b/solution.py
@@ -23,7 +23,7 @@
 
 def dot_t(a, b):
     return lax.dot_general(a, b, (((1,), (1,)), ((), ())), preferred_element_type=f32)
-LONG = (2, 5)
+LONG = ()
 
 
 def dot_c(a, b):
@@ -91,7 +91,7 @@
     scale, key_n, head_n, rows, tile, block, group,
     e_hbm, dp_hbm, qc_hbm, dl_hbm, lt_hbm, uk_hbm, st_ref, tops_ref,
     out_ref, dqo_ref,
-    e_ref, dp_ref, qc_ref, dl_ref, lt_ref, uk_ref, norm_ref, delta_ref, part_ref, got_ref,
+    e_ref, dp_ref, qc_ref, dl_ref, lt_ref, uk_ref, norm_ref, delta_ref, part_ref, got_ref, gat_ref,
     dq_ref, dqg_ref, stg_ref,
     e_sem, dp_sem, in_sem, st_send, st_recv, rs_send, rs_recv, ag_send, ag_recv, q_send, q_recv,
 ):
@@ -197,8 +197,7 @@
         if b == 0:
             weights[0].wait()
             weights[1].wait()
-        if b + 1 < blocks:
-            prepare(b + 1)
+        prepare(b)
         at = pl.ds(b * block, block)
         from_scores = dot_t(qc_ref[...], dp_ref[at, :]) * scale
         from_values = dot_t(dl_ref[...], e_ref[at, :])
@@ -254,7 +253,7 @@
             for j in range(size):
                 summed = part_ref[b, base[b] + j].astype(f32) + got_ref[b, spot + j].astype(f32)
                 if k == bits:
-                    out_ref[base[b] + j, :, b * block : (b + 1) * block] = summed.astype(bf16)
+                    gat_ref[b, base[b] + j] = summed.astype(bf16)
                 else:
                     part_ref[b, base[b] + j] = summed.astype(bf16)
         if k < bits:
@@ -272,11 +271,14 @@
             size = 1 << i
             if i > 0:
                 base[b] = base[b] - bit(order[bits - i]) * (size // 2)
-            at = out_ref.at[pl.ds(base[b], size), :, pl.ds(b * block, block)]
+            at = gat_ref.at[b, pl.ds(base[b], size)]
             flight[b] = remote(
                 at, at,
                 ag_send.at[b, i], ag_recv.at[b, i], {"head": partner(order[bits - 1 - i])},
             )
+        elif k == 2 * bits:
+            for j in range(head_n):
+                out_ref[j, :, b * block : (b + 1) * block] = gat_ref[b, j]
         stage[b] = k + 1
 
     age = [0] * blocks
@@ -291,9 +293,7 @@
                     age[b] = 0
 
     work = [(latent_block, b) for b in range(blocks)]
-    work = work[:-1] + [(query_group, 0)] + work[-1:]
-    work += [(query_group, g) for g in range(1, groups)]
-    prepare(0)
+    work += [(query_group, g) for g in range(groups)]
     for do, i in work:
         do(i)
         if do is latent_block:
@@ -390,6 +390,7 @@
             pltpu.VMEM((heads, rows), f32),
             pltpu.VMEM((blocks, head_n, piece, block), bf16),
             pltpu.VMEM((blocks, head_n, piece, block), bf16),
+            pltpu.VMEM((blocks, head_n, piece, block), bf16),
             pltpu.VMEM((key_n, groups, slots, chunk, nope), bf16),
             pltpu.VMEM((key_n - 1, groups, slots, chunk, nope), bf16),
             pltpu.VMEM((key_n - 1, 3, heads, rows), f32),

time: 88.1 us -> 80.1 us (0.909)
  Pallas kernels: 80 us -> 72.1 us
    pallas_call x1, Pallas kernels: 59 us -> 51 us  [shards(): pl.pallas_call(functools.partial(grads_kernel, scale, key_n, head_n, rows...]
where the time goes in v4:
time: 80.1 us; the launch traced here: 79.8 us
  Pallas kernels  72.1 us (90%)
  local copies, waits for them, and re-layouts  7.12 us (9%)
    pallas_call x1, Pallas kernels, shards(): pl.pallas_call(functools.partial(grads_kernel, scale, key_n, head_n, rows...  51 us
    pallas_call x1, Pallas kernels, shards(): pl.pallas_call(functools.partial(scores_kernel, scale, group, tile), grid...  21 us
    unnamed x2, local copies, waits for them, and re-layouts  5.32 us
    reshape x1, local copies, waits for them, and re-layouts, shards(): return (dq.reshape(heads, chunk, width).transpose(1, 0, 2), d_latent)  1.8 us

profile of v4, /device:TPU:0, one launch (start us, length us, event | category | flops | bytes accessed | tf_op | source)
XLA Modules:
  0.0 79.8 jit_solution(3580155920292430254)
XLA Ops:
  0.6 2.0 %copy.12 = bf16[128,16,128]{2,0,1:T(8,128)(2,1)} copy(bf16[128,16,128]{2,1,0:T(8,128)(2,1)} %param.10) | data formatting | bytes 1048576 | tf_op args[4]
  2.6 21.0 %shard_map.77 = (bf16[2048,2048]{1,0:T(8,128)(2,1)}, bf16[2048,2048]{1,0:T(8,128)(2,1)}, bf16[576,2048]{1,0:T(8,128)(2,1)}, bf16[512,2048]{1,0:T(8,128)(2,1)}, f...) custom-call(bf16[16,192,128]{2,1,0:T(8,128)(2,1)} %bitcast.17, bf16[16,128,128]{2,1,0:T(8,128)(2,1)} %bitcast.16, ...), custom_call_target="tpu_custom_call" | custom-call | tf_op jit(solution)/shard_map/pallas_call | solution.py:338
  23.6 51.0 %shard_map.78 = (bf16[8,72,2048]{2,1,0:T(8,128)(2,1)}, bf16[4,4,32,192]{3,2,1,0:T(8,128)(2,1)}) custom-call(bf16[2048,2048]{1,0:T(8,128)(2,1)} %get-tuple-element.10.e_hbm, bf16[2048,2048]{1,0:T(8,128)(2,1)} %get-tuple-element.11.dp_hbm, bf16[576,2048]{1,0:T(8,128)(2,1)} %get-tuple-element.12.qc_hbm, bf16[512,2048]{1,0:T(8,128)(2,1)} %get-tuple-element.13.dl_hbm, ...), custom_call_target="tpu_custom_call" | custom-call | tf_op jit(solution)/shard_map/pallas_call | solution.py:374
  74.7 1.8 %copy.13 = bf16[16,32,192]{2,0,1:T(8,128)(2,1)} copy(bf16[16,32,192]{2,1,0:T(8,128)(2,1)} %bitcast.19) | data formatting | bytes 393216 | tf_op jit(solution)/shard_map/reshape | solution.py:414
  76.5 3.4 %copy.15 = bf16[2048,576]{0,1:T(8,128)(2,1)} copy(bf16[2048,576]{0,1:T(8,128)(2,1)} %bitcast.15) | data formatting | bytes 4718592
